TPU v7x, 512 devices: a whole 4x8x8 slice. The times are simulated.
512 devices in a mesh: tok: 64 (over z, y_hi, x), feat: 8 (over y_lo, core).
Axes of the slice: x: 4, y: 8 (y_hi: 2, y_lo: 4; y = y_hi * 4 + y_lo), z: 8, core: 2. Of those that a mesh axis runs over, the one named last changes fastest.
Arguments:
- activations: bfloat16 [131072, 8192], P('tok', 'feat')
- labels: int32 [131072], P('tok'), may hold values from 0 to 7, as said below
Outputs:
- cov_panel: float32 [1024, 8192], P('tok', 'feat')
- cross_cov: float32 [8, 8192], P(None, 'feat')
Inputs may be any that keep to these rules, and one draw needn't show every extreme that they name: `labels`: each token's class.
All inputs are finite; a program needn't handle non-finite values.
Results may differ from a plain program's by a relative error of at most 0.0017.
Values may be sent and summed in bfloat16 or wider, within the bound.
A program may use at most 64 MiB of HBM per device.

v0:
```python
import jax
import jax.numpy as jnp
from jax import lax
from jax.sharding import PartitionSpec as P

CLASSES = 8
PANEL = 128


def tokens_product(left, right):
    return lax.dot_general(
        left, right, (((0,), (0,)), ((), ())), preferred_element_type=jnp.float32
    )


def body(activations, labels):
    tok_rows = activations.shape[0]
    total = tok_rows * lax.axis_size("tok")
    column_total = lax.psum(jnp.sum(activations, axis=0, dtype=jnp.float32), "tok")
    mean = column_total / total
    centered = (activations.astype(jnp.float32) - mean).astype(jnp.bfloat16)
    onehot = (labels[:, None] == jnp.arange(CLASSES, dtype=jnp.int32)[None, :]).astype(jnp.bfloat16)
    class_part = tokens_product(onehot, centered)
    class_total = lax.psum(class_part, "tok")
    cross_cov = class_total / total
    outgoing = centered[:, :PANEL]
    panel = lax.all_gather(outgoing, "feat", axis=1, tiled=True)
    summed = lax.psum_scatter(
        tokens_product(panel, centered), "tok", scatter_dimension=0, tiled=True
    )
    cov_panel = summed / (total - 1)
    return (cov_panel, cross_cov)


def solution(mesh):
    in_specs = (P("tok", "feat"), P("tok"))
    out_specs = (P("tok", "feat"), P(None, "feat"))
    return jax.shard_map(body, mesh=mesh, in_specs=in_specs, out_specs=out_specs, check_vma=False)
```

profile of v0, /device:TPU:8, one launch (start us, length us, event | category | flops | bytes accessed | tf_op | source)
XLA Modules:
  0.0 762.9 jit_solution(16792029753697239541)
XLA Ops:
  7.2 0.0 all-gather.2.cloned.1.call-start
  7.2 2.9 convert_reduce_fusion
  10.1 230.5 %psum.14 = f32[1024]{0:T(1024)S(1)} all-reduce(f32[1024]{0:T(1024)S(1)} %convert_reduce_fusion), channel_id=1, replica_groups=mesh['tok'=64,'feat'=8] {'tok'}, use_global_device_ids=true, to_apply=%region_1.0 | all-reduce | flops 1024 | bytes 8192 | tf_op jit(solution)/shard_map/psum | solution.py:19
  240.5 3.3 fusion
  243.9 0.0 copy-start
  243.9 1.9 copy-done
  245.8 0.9 slice.4
  246.7 0.0 all-gather.2.cloned.1.call-update
  246.8 0.0 reduce-scatter.2.cloned.1.call-start
  246.8 45.1 %all-gather.2.cloned.1.call-done = bf16[2048,1024]{1,0:T(8,128)(2,1)} async-done(((bf16[2048,128]{1,0:T(8,128)(2,1)}), bf16[2048,1024]{1,0:T(8,128)(2,1)}) %all-gather.2.cloned.1.call-update) | async-done | bytes 4194320 | tf_op jit(solution)/shard_map/all_gather | solution.py:27
  291.9 10.0 %fusion.3 = f32[1024,1024]{1,0:T(8,128)} fusion(bf16[2048,1024]{1,0:T(8,128)(2,1)} %all-gather.2.cloned.1.call-done, bf16[2048,1024]{1,0:T(8,128)(2,1)} %copy-done), kind=kOutput, calls=%fused_computation.9 | convolution fusion | flops 4294967296 | bytes 12582912 | tf_op jit(solution)/shard_map/dot_general | solution.py:11
  301.9 0.0 copy-start.1
  301.9 0.0 reduce-scatter.2.cloned.1.call-update
  301.9 0.7 copy-done.1
  302.6 3.1 fusion.1
  305.7 437.9 %psum.15 = f32[8,1024]{1,0:T(8,128)S(1)} all-reduce(f32[8,1024]{1,0:T(8,128)S(1)} %fusion.1), channel_id=1, replica_groups=mesh['tok'=64,'feat'=8] {'tok'}, use_global_device_ids=true, to_apply=%region_3.0 | all-reduce | flops 8192 | bytes 65536 | tf_op jit(solution)/shard_map/psum | solution.py:24
  743.7 0.6 broadcast_multiply_fusion.1
  744.3 10.3 %reduce-scatter.2.cloned.1.call-done = f32[16,1024]{1,0:T(8,128)} async-done(((f32[1024,1024]{1,0:T(8,128)}), f32[16,1024]{1,0:T(8,128)}) %reduce-scatter.2.cloned.1.call-update) | async-done | bytes 65552 | tf_op jit(solution)/shard_map/reduce_scatter | solution.py:28
  754.6 1.5 broadcast_multiply_fusion
  (1 shorter events, 0.0 us)
Async XLA Ops:
  7.2 284.7 %all-gather.2.cloned.1.call-start = ((), (), s32[]{:S(2)}) async-start(), calls=%async_computation.1 | async-start | bytes 4718592 | tf_op jit(solution)/shard_map/all_gather | solution.py:27
  243.9 1.9 copy-start
  246.8 507.8 %reduce-scatter.2.cloned.1.call-start = ((), (), s32[]{:S(2)}) async-start(), calls=%async_computation.2 | async-start | bytes 4259840 | tf_op jit(solution)/shard_map/reduce_scatter | solution.py:28
  301.9 0.7 copy-start.1
Sparse Core Ops, SparseCore 0:
  246.9 44.9 all-gather.1
  302.0 452.4 reduce-scatter.1
where the time goes:
time: 763 us
  blocking collectives  668 us (88%)
  waiting for transfers between devices  55.4 us (7%)
  between operations  14.1 us (2%)
  matrix products  13.1 us (2%)
  other arithmetic  8.3 us (1%)
    psum x1, blocking collectives, body(): class_total = lax.psum(class_part, 'tok')  438 us
    psum x1, blocking collectives, body(): lax.psum(jnp.sum(activations, axis=0, dtype=jnp.float32), 'tok')  230 us
    all_gather x1, waiting for transfers between devices, body(): panel = lax.all_gather(outgoing, 'feat', axis=1, tiled=True)  45.1 us
  transfers between devices with their start and end apart: 2, of which 2 were waited for; matrix products, arithmetic and copies ran while one was open for 0% of the time, Pallas kernels for 0%

commit v1 on v0

--- a/solution.py
+++ b/solution.py
@@ -5,6 +5,11 @@
 
 CLASSES = 8
 PANEL = 128
+
+
+def gather_over(x, axis, dim):
+    sent = jnp.stack([x] * lax.axis_size(axis))
+    return jnp.concatenate(lax.all_to_all(sent, axis, 0, 0), axis=dim)
 
 
 def tokens_product(left, right):
@@ -24,7 +29,7 @@
     class_total = lax.psum(class_part, "tok")
     cross_cov = class_total / total
     outgoing = centered[:, :PANEL]
-    panel = lax.all_gather(outgoing, "feat", axis=1, tiled=True)
+    panel = gather_over(outgoing, "feat", 1)
     summed = lax.psum_scatter(
         tokens_product(panel, centered), "tok", scatter_dimension=0, tiled=True
     )

time: 763 us -> 800 us (1.048)
  blocking collectives: 668 us -> 755 us
  waiting for transfers between devices: 55.4 us -> 8.65 us
    all_to_all x0 -> x1, blocking collectives: none -> 95.6 us  [gather_over(): return jnp.concatenate(lax.all_to_all(sent, axis, 0, 0), axis=dim)]
    all_gather x1 -> x0, waiting for transfers between devices: 45.1 us -> none  [body(): panel = lax.all_gather(outgoing, 'feat', axis=1, tiled=True)]
    psum x1, blocking collectives: 438 us -> 429 us  [body(): class_total = lax.psum(class_part, 'tok')]
  transfers between devices with their start and end apart: 2 -> 1, of which waited for: 2 -> 1; matrix products, arithmetic and copies ran while one was open for 0% -> 0% of each run, Pallas kernels for 0% -> 0%
where the time goes in v1:
time: 800 us; the launch traced here: 799 us
  blocking collectives  755 us (94%)
  between operations  14.1 us (2%)
  matrix products  9.18 us (1%)
  waiting for transfers between devices  8.65 us (1%)
  other arithmetic  8.3 us (1%)
    psum x1, blocking collectives, body(): class_total = lax.psum(class_part, 'tok')  429 us
    psum x1, blocking collectives, body(): lax.psum(jnp.sum(activations, axis=0, dtype=jnp.float32), 'tok')  231 us
    all_to_all x1, blocking collectives, gather_over(): return jnp.concatenate(lax.all_to_all(sent, axis, 0, 0), axis=dim)  95.6 us
  transfers between devices with their start and end apart: 1, of which 1 were waited for; matrix products, arithmetic and copies ran while one was open for 0% of the time, Pallas kernels for 0%

profile of v1, /device:TPU:8, one launch (start us, length us, event | category | flops | bytes accessed | tf_op | source)
XLA Modules:
  0.0 799.2 jit_solution(10261682642671693419)
XLA Ops:
  7.2 0.0 reduce-scatter.2.cloned.1.call-start
  7.2 2.9 convert_reduce_fusion
  10.1 230.6 %psum.14 = f32[1024]{0:T(1024)S(1)} all-reduce(f32[1024]{0:T(1024)S(1)} %convert_reduce_fusion), channel_id=1, replica_groups=mesh['tok'=64,'feat'=8] {'tok'}, use_global_device_ids=true, to_apply=%region_1.0 | all-reduce | flops 1024 | bytes 8192 | tf_op jit(solution)/shard_map/psum | solution.py:24
  240.6 3.3 fusion
  244.0 0.0 copy-start
  244.0 1.9 copy-done
  245.9 0.1 slice.4
  246.1 0.2 copy.4
  246.3 0.5 stack.2
  246.8 0.0 copy-start.1
  246.8 95.6 %all_to_all.5 = bf16[8,2048,128]{1,2,0:T(8,128)(2,1)S(1)} all-to-all(bf16[8,2048,128]{1,2,0:T(8,128)(2,1)S(1)} %stack.2), channel_id=1, replica_groups=mesh['tok'=64,'feat'=8] {'feat'}, dimensions={0} | all-to-all | bytes 8388608 | tf_op jit(solution)/shard_map/all_to_all | solution.py:12
  342.4 0.0 copy-done.1
  342.4 6.0 fusion.3
  348.5 0.0 copy-start.2
  348.5 0.0 reduce-scatter.2.cloned.1.call-update
  348.5 0.7 copy-done.2
  349.2 3.1 fusion.1
  352.3 429.3 %psum.15 = f32[8,1024]{1,0:T(8,128)S(1)} all-reduce(f32[8,1024]{1,0:T(8,128)S(1)} %fusion.1), channel_id=1, replica_groups=mesh['tok'=64,'feat'=8] {'tok'}, use_global_device_ids=true, to_apply=%region_3.0 | all-reduce | flops 8192 | bytes 65536 | tf_op jit(solution)/shard_map/psum | solution.py:29
  781.6 0.6 broadcast_multiply_fusion.1
  782.2 8.6 %reduce-scatter.2.cloned.1.call-done = f32[16,1024]{1,0:T(8,128)} async-done(((f32[1024,1024]{1,0:T(8,128)}), f32[16,1024]{1,0:T(8,128)}) %reduce-scatter.2.cloned.1.call-update) | async-done | bytes 65552 | tf_op jit(solution)/shard_map/reduce_scatter | solution.py:33
  790.9 1.5 broadcast_multiply_fusion
  (1 shorter events, 0.0 us)
Async XLA Ops:
  7.2 783.7 %reduce-scatter.2.cloned.1.call-start = ((), (), s32[]{:S(2)}) async-start(), calls=%async_computation.2 | async-start | bytes 4259840 | tf_op jit(solution)/shard_map/reduce_scatter | solution.py:33
  244.0 1.9 copy-start
  246.8 95.6 %copy-start.1 = (bf16[2048,1024]{1,0:T(8,128)(2,1)S(1)}, bf16[2048,1024]{1,0:T(8,128)(2,1)}, u32[]{:S(2)}) copy-start(bf16[2048,1024]{1,0:T(8,128)(2,1)} %copy-done) | copy-start | bytes 12582916
  348.5 0.7 copy-start.2
Sparse Core Ops, SparseCore 0:
  348.6 442.2 reduce-scatter.1
